TPU v7x, 128 devices: a whole 4x4x4 slice. The times are simulated.
128 devices in a mesh: dp: 16 (over y, z_lo, core), mp: 8 (over z_hi, x).
Axes of the slice: x: 4, y: 4, z: 4 (z_hi: 2, z_lo: 2; z = z_hi * 2 + z_lo), core: 2. Of those that a mesh axis runs over, the one named last changes fastest.
Arguments:
- doc_ids: int32 [16, 512], P('dp'), may hold values from 0 to 128255
- doc_lengths: int32 [16], P('dp'), may hold values from 128 to 512
- activations: bfloat16 [8192, 4096], P('dp'), may hold values from -6 to 6
- out_grads: bfloat16 [8192, 14336], P('dp'), may hold values from -0.29882812 to 0.29882812
- input_basis: bfloat16 [4096, 2048], P(None, 'mp'), may hold values from -0.09375 to 0.09375
- output_basis: bfloat16 [14336, 7168], P('dp', 'mp'), may hold values from -0.046875 to 0.046875
- eigenvalues: bfloat16 [2048, 7168], P(None, 'mp'), may hold values from 0.5 to 50
- query_left: bfloat16 [64, 32, 2048], P('dp'), may hold values from -0.125 to 0.125
- query_right: bfloat16 [64, 32, 7168], P('dp', None, 'mp'), may hold values from -0.0625 to 0.0625
Outputs:
- scores: float32 [16, 64], P('dp')
Inputs may be any that keep to these rules, and one draw needn't show every extreme that they name: `doc_lengths`: the live tokens are the first ones of each document.
All inputs are finite; a program needn't handle non-finite values.
Results may differ from a plain program's by a relative error of at most 0.023.
Values may be sent and summed in bfloat16 or wider, within the bound.
No kernel may reach another device: no remote copies, remote signals or barrier semaphores. Data moves between devices by JAX's collectives and lax.ppermute only.
A program may use at most 192 MiB of HBM per device.

v0:
```python
import jax
import jax.numpy as jnp
from jax import lax
from jax.sharding import PartitionSpec as P

damping = 0.5


def laid_out(blocks, dim):
    blocks = jnp.moveaxis(blocks, 0, dim)
    dims = blocks.shape
    return blocks.reshape(*dims[:dim], dims[dim] * dims[dim + 1], *dims[dim + 2 :])


def from_everyone(array, axis):
    length = lax.axis_size(axis)
    return lax.all_to_all(
        jnp.broadcast_to(array[None], (length, *array.shape)), axis, 0, 0, tiled=True
    )


def gather_directly(array, axis, dim):
    return laid_out(from_everyone(array, axis), dim)


def taken_together(array, axis):
    everything = from_everyone(array, axis)
    return jnp.sum(everything, axis=0)


def token_weights(doc_ids, doc_lengths):
    positions = jnp.arange(doc_ids.shape[1], dtype=jnp.int32)
    active = positions[None, :] < doc_lengths[:, None]
    matches = (doc_ids[:, :, None] == doc_ids[:, None, :]) & active[:, None, :]
    repeats = jnp.sum(matches.astype(jnp.float32), axis=2)
    return jnp.where(active, 1.0 / jnp.maximum(repeats, 1.0), 0.0)


def per_device(
    doc_ids,
    doc_lengths,
    activations,
    out_grads,
    input_basis,
    output_basis,
    eigenvalues,
    query_left,
    query_right,
):
    tok_rows = activations.shape[0]
    shard_rows = output_basis.shape[0]
    out_cols = output_basis.shape[1]
    rotated_share = jnp.dot(activations, input_basis, preferred_element_type=jnp.float32).astype(
        jnp.bfloat16
    )
    rotated_in = gather_directly(rotated_share, "mp", 1)
    empty = jnp.zeros((tok_rows, out_cols), jnp.float32)
    running = empty
    pieces = lax.all_gather(output_basis, "dp", axis=0, tiled=True)
    for member in range(pieces.shape[0] // shard_rows):
        grad_cols = lax.dynamic_slice_in_dim(out_grads, member * shard_rows, shard_rows, 1)
        partial_value = jnp.dot(
            grad_cols,
            pieces[member * shard_rows : (member + 1) * shard_rows],
            preferred_element_type=jnp.float32,
        )
        running = running + lax.optimization_barrier(partial_value.astype(jnp.bfloat16)).astype(
            jnp.float32
        )
    rotated_out = running.astype(jnp.bfloat16)
    weights = token_weights(doc_ids, doc_lengths)
    docs_here = doc_ids.shape[0]
    acts_doc = rotated_in.reshape(docs_here, -1, rotated_in.shape[1])
    grads_doc = rotated_out.reshape(docs_here, -1, out_cols)
    scaled = (weights[:, :, None] * grads_doc.astype(jnp.float32)).astype(jnp.bfloat16)
    gradient = jnp.einsum("dti,dtj->dij", acts_doc, scaled, preferred_element_type=jnp.float32)
    conditioned = (gradient / (eigenvalues.astype(jnp.float32) + damping)).astype(jnp.bfloat16)
    rank_rows = query_left.shape[1]
    left_part = lax.all_gather(query_left, "dp", axis=0, tiled=True)
    right_part = lax.all_gather(query_right, "dp", axis=0, tiled=True)
    number = left_part.shape[0]
    left_rows = left_part.reshape(number * rank_rows, left_part.shape[2])
    right_rows = right_part.reshape(number * rank_rows, right_part.shape[2]).astype(jnp.float32)
    mixture = jnp.einsum("ri,dij->drj", left_rows, conditioned, preferred_element_type=jnp.float32)
    values = jnp.sum((mixture * right_rows[None]).reshape(docs_here, number, -1), axis=2)
    return taken_together(values, "mp")


def solution(mesh):
    return jax.shard_map(
        per_device,
        mesh=mesh,
        in_specs=(
            P("dp", None),
            P("dp"),
            P("dp", None),
            P("dp", None),
            P(None, "mp"),
            P("dp", "mp"),
            P(None, "mp"),
            P("dp", None, None),
            P("dp", None, "mp"),
        ),
        out_specs=P("dp", None),
        check_vma=False,
    )
```

profile of v0, /device:TPU:0, one launch (start us, length us, event | category | flops | bytes accessed | tf_op | source)
XLA Modules:
  0.0 307.4 jit_solution(3509372564559330316)
XLA Ops:
  6.5 0.0 copy-start
  6.5 0.0 all-gather.8.cloned.1.call-start
  6.5 0.7 all-gather.8.cloned.1.call-update
  7.3 0.0 all-gather.4.cloned.1.call-start
  7.3 0.7 all-gather.4.cloned.1.call-update
  8.0 0.0 all-gather.6.cloned.1.call-start
  8.1 0.7 all-gather.6.cloned.1.call-update
  8.7 0.0 copy-done
  8.8 3.4 %convolution_convert_fusion = bf16[512,256]{1,0:T(8,128)(2,1)S(1)} fusion(bf16[512,4096]{1,0:T(8,128)(2,1)} %param.11, bf16[4096,256]{1,0:T(8,128)(2,1)S(1)} %copy-done), kind=kOutput, calls=%fused_computation.56 | convolution fusion | flops 1073872896 | bytes 6553600 | tf_op jit(solution)/shard_map/dot_general | solution.py:53
  12.2 0.1 copy.17
  12.3 1.5 broadcast_in_dim.7
  13.8 0.0 copy-start.2
  13.8 7.8 %all-to-all-start = ((bf16[8,512,256]{1,2,0:T(8,128)(2,1)}), bf16[8,512,256]{1,2,0:T(8,128)(2,1)}, u32[]{:S(2)}, u32[]{:S(2)}) async-start(bf16[8,512,256]{1,2,0:T(8,128)(2,1)} %broadcast_in_dim.7), calls=%async_computation | async-start | bytes 4194304 | tf_op jit(solution)/shard_map/all_to_all | solution.py:17
  22.3 0.0 copy-done.2
  22.3 0.3 convert_reduce_fusion
  22.7 46.0 %all-gather.8.cloned.1.call-done = bf16[64,32,896]{2,1,0:T(8,128)(2,1)} async-done(((bf16[4,32,896]{2,1,0:T(8,128)(2,1)}), bf16[64,32,896]{2,1,0:T(8,128)(2,1)}) %all-gather.8.cloned.1.call-update) | async-done | bytes 3670032 | tf_op jit(solution)/shard_map/all_gather | solution.py:80
  68.6 5.5 %bitcast_convert_fusion = f32[1,2048,896]{2,1,0:T(8,128)} fusion(bf16[1,2048,896]{2,1,0:T(8,128)(2,1)} %bitcast.24), kind=kLoop, calls=%fused_computation.3 | loop fusion | flops 1835008 | bytes 11010048 | tf_op jit(solution)/shard_map/convert_element_type | solution.py:83
  74.1 8.7 %copy.18 = f32[1,2048,896]{1,2,0:T(8,128)} copy(f32[1,2048,896]{2,1,0:T(8,128)} %bitcast_convert_fusion) | data formatting | bytes 14680064 | tf_op jit(solution)/shard_map/convert_element_type | solution.py:83
  82.8 121.5 %all-gather.4.cloned.1.call-done = bf16[14336,896]{1,0:T(8,128)(2,1)} async-done(((bf16[896,896]{1,0:T(8,128)(2,1)}), bf16[14336,896]{1,0:T(8,128)(2,1)}) %all-gather.4.cloned.1.call-update) | async-done | bytes 25690128 | tf_op jit(solution)/shard_map/all_gather | solution.py:59
  204.3 0.0 copy-start.3
  204.3 3.1 fusion.36
  207.4 4.6 %fusion.39 = bf16[512,896]{1,0:T(8,128)(2,1)} fusion(bf16[14336,896]{1,0:T(8,128)(2,1)} %all-gather.4.cloned.1.call-done, bf16[512,14336]{1,0:T(8,128)(2,1)} %param.12), kind=kOutput, calls=%fused_computation.41 | convolution fusion | flops 822542336 | bytes 3440640 | tf_op jit(solution)/shard_map/dot_general | solution.py:62
  212.0 4.6 %fusion.42 = bf16[512,896]{1,0:T(8,128)(2,1)} fusion(bf16[14336,896]{1,0:T(8,128)(2,1)} %all-gather.4.cloned.1.call-done, bf16[512,14336]{1,0:T(8,128)(2,1)} %param.12), kind=kOutput, calls=%fused_computation.42 | convolution fusion | flops 822542336 | bytes 3440640 | tf_op jit(solution)/shard_map/dot_general | solution.py:62
  216.6 3.8 %fusion.45 = bf16[512,896]{1,0:T(8,128)(2,1)} fusion(bf16[14336,896]{1,0:T(8,128)(2,1)} %all-gather.4.cloned.1.call-done, bf16[512,14336]{1,0:T(8,128)(2,1)} %param.12), kind=kOutput, calls=%fused_computation.43 | convolution fusion | flops 822542336 | bytes 3440640 | tf_op jit(solution)/shard_map/dot_general | solution.py:62
  220.5 3.9 %fusion.48 = bf16[512,896]{1,0:T(8,128)(2,1)} fusion(bf16[14336,896]{1,0:T(8,128)(2,1)} %all-gather.4.cloned.1.call-done, bf16[512,14336]{1,0:T(8,128)(2,1)} %param.12), kind=kOutput, calls=%fused_computation.44 | convolution fusion | flops 822542336 | bytes 3440640 | tf_op jit(solution)/shard_map/dot_general | solution.py:62
  224.4 0.0 copy-done.3
  224.4 3.4 %fusion.51 = bf16[512,896]{1,0:T(8,128)(2,1)} fusion(bf16[14336,896]{1,0:T(8,128)(2,1)S(1)} %copy-done.3, bf16[512,14336]{1,0:T(8,128)(2,1)} %param.12), kind=kOutput, calls=%fused_computation.45 | convolution fusion | flops 822542336 | bytes 3440640 | tf_op jit(solution)/shard_map/dot_general | solution.py:62
  227.7 3.3 %fusion.54 = bf16[512,896]{1,0:T(8,128)(2,1)} fusion(bf16[14336,896]{1,0:T(8,128)(2,1)S(1)} %copy-done.3, bf16[512,14336]{1,0:T(8,128)(2,1)} %param.12), kind=kOutput, calls=%fused_computation.46 | convolution fusion | flops 822542336 | bytes 3440640 | tf_op jit(solution)/shard_map/dot_general | solution.py:62
  231.1 3.4 %fusion.57 = bf16[512,896]{1,0:T(8,128)(2,1)} fusion(bf16[14336,896]{1,0:T(8,128)(2,1)S(1)} %copy-done.3, bf16[512,14336]{1,0:T(8,128)(2,1)} %param.12), kind=kOutput, calls=%fused_computation.47 | convolution fusion | flops 822542336 | bytes 3440640 | tf_op jit(solution)/shard_map/dot_general | solution.py:62
  234.4 3.4 %fusion.60 = bf16[512,896]{1,0:T(8,128)(2,1)} fusion(bf16[14336,896]{1,0:T(8,128)(2,1)S(1)} %copy-done.3, bf16[512,14336]{1,0:T(8,128)(2,1)} %param.12), kind=kOutput, calls=%fused_computation.48 | convolution fusion | flops 822542336 | bytes 3440640 | tf_op jit(solution)/shard_map/dot_general | solution.py:62
  237.8 3.3 %fusion.63 = bf16[512,896]{1,0:T(8,128)(2,1)} fusion(bf16[14336,896]{1,0:T(8,128)(2,1)S(1)} %copy-done.3, bf16[512,14336]{1,0:T(8,128)(2,1)} %param.12), kind=kOutput, calls=%fused_computation.49 | convolution fusion | flops 822542336 | bytes 3440640 | tf_op jit(solution)/shard_map/dot_general | solution.py:62
  241.1 3.4 %fusion.66 = bf16[512,896]{1,0:T(8,128)(2,1)} fusion(bf16[14336,896]{1,0:T(8,128)(2,1)S(1)} %copy-done.3, bf16[512,14336]{1,0:T(8,128)(2,1)} %param.12), kind=kOutput, calls=%fused_computation.50 | convolution fusion | flops 822542336 | bytes 3440640 | tf_op jit(solution)/shard_map/dot_general | solution.py:62
  244.5 3.3 %fusion.69 = bf16[512,896]{1,0:T(8,128)(2,1)} fusion(bf16[14336,896]{1,0:T(8,128)(2,1)S(1)} %copy-done.3, bf16[512,14336]{1,0:T(8,128)(2,1)} %param.12), kind=kOutput, calls=%fused_computation.51 | convolution fusion | flops 822542336 | bytes 3440640 | tf_op jit(solution)/shard_map/dot_general | solution.py:62
  247.8 3.3 %fusion.72 = bf16[512,896]{1,0:T(8,128)(2,1)} fusion(bf16[14336,896]{1,0:T(8,128)(2,1)S(1)} %copy-done.3, bf16[512,14336]{1,0:T(8,128)(2,1)} %param.12), kind=kOutput, calls=%fused_computation.52 | convolution fusion | flops 822542336 | bytes 3440640 | tf_op jit(solution)/shard_map/dot_general | solution.py:62
  251.1 3.6 %fusion.75 = bf16[512,896]{1,0:T(8,128)(2,1)} fusion(bf16[14336,896]{1,0:T(8,128)(2,1)S(1)} %copy-done.3, bf16[512,14336]{1,0:T(8,128)(2,1)} %param.12), kind=kOutput, calls=%fused_computation.53 | convolution fusion | flops 822542336 | bytes 3440640 | tf_op jit(solution)/shard_map/dot_general | solution.py:62
  254.7 3.3 %fusion.78 = bf16[512,896]{1,0:T(8,128)(2,1)} fusion(bf16[14336,896]{1,0:T(8,128)(2,1)S(1)} %copy-done.3, bf16[512,14336]{1,0:T(8,128)(2,1)} %param.12), kind=kOutput, calls=%fused_computation.54 | convolution fusion | flops 822542336 | bytes 3440640 | tf_op jit(solution)/shard_map/dot_general | solution.py:62
  258.1 3.3 %fusion.81 = bf16[512,896]{1,0:T(8,128)(2,1)} fusion(bf16[14336,896]{1,0:T(8,128)(2,1)S(1)} %copy-done.3, bf16[512,14336]{1,0:T(8,128)(2,1)} %param.12), kind=kOutput, calls=%fused_computation.55 | convolution fusion | flops 822542336 | bytes 3440640 | tf_op jit(solution)/shard_map/dot_general | solution.py:62
  261.4 0.0 all-to-all-done
  261.4 0.0 all-gather.6.cloned.1.call-done
  261.4 0.0 copy-start.1
  261.4 24.7 %fusion = f32[2048]{0:T(1024)S(1)} fusion(f32[1,2048,896]{1,2,0:T(8,128)} %copy.18, bf16[2048,2048]{1,0:T(8,128)(2,1)} %bitcast.27, bf16[2048,896]{1,0:T(8,128)(2,1)} %param.15, bf16[512,2048]{0,1:T(8,128)(2,1)} %bitcast.1, f32[512]{0:T(512)S(1)} %divide_select_fusion, bf16[512,896]{1,0:T(8,128)(2,1)} %fusion.81, bf16[512,896]{1,0:T(8,128)(2,1)} %fusion.78, ...), kind=kOutput, calls=%fused_computation.1 | convolution fusion | flops 9422305280 | bytes 36186112 | tf_op jit(solution)/shard_map/ri,dij->drj/dot_general | solution.py:84
  286.1 0.1 reduce_sum.38
  286.1 0.1 reduce_sum.39
  286.3 14.0 %all_to_all.10 = f32[8,1,64]{2,1,0:T(1,128)S(1)} all-to-all(f32[8,1,64]{2,1,0:T(1,128)S(1)} %broadcast_in_dim.9), channel_id=1, replica_groups=mesh['dp'=16,'mp'=8] {'mp'}, dimensions={0} | all-to-all | bytes 4096 | tf_op jit(solution)/shard_map/all_to_all | solution.py:17
  300.3 0.5 reduce_sum.40
  300.8 0.0 copy-done.1
  (3 shorter events, 0.0 us)
Async XLA Ops:
  6.5 2.2 copy-start
  6.5 62.1 %all-gather.8.cloned.1.call-start = ((), (), s32[]{:S(2)}) async-start(), calls=%async_computation.4 | async-start | bytes 3899392 | tf_op jit(solution)/shard_map/all_gather | solution.py:80
  7.3 197.1 %all-gather.4.cloned.1.call-start = ((), (), s32[]{:S(2)}) async-start(), calls=%async_computation.2 | async-start | bytes 27295744 | tf_op jit(solution)/shard_map/all_gather | solution.py:59
  8.0 253.4 %all-gather.6.cloned.1.call-start = ((), (), s32[]{:S(2)}) async-start(), calls=%async_computation.3 | async-start | bytes 8912896 | tf_op jit(solution)/shard_map/all_gather | solution.py:79
  13.8 8.5 %copy-start.2 = (s32[1,512]{1,0:T(1,128)S(1)}, s32[1,512]{1,0:T(1,128)}, u32[]{:S(2)}) copy-start(s32[1,512]{1,0:T(1,128)} %param.9) | copy-start | bytes 6148
  13.8 247.6 %all-to-all-start = ((bf16[8,512,256]{1,2,0:T(8,128)(2,1)}), bf16[8,512,256]{1,2,0:T(8,128)(2,1)}, u32[]{:S(2)}, u32[]{:S(2)}) async-start(bf16[8,512,256]{1,2,0:T(8,128)(2,1)} %broadcast_in_dim.7), calls=%async_computation | async-start | bytes 4194304 | tf_op jit(solution)/shard_map/all_to_all | solution.py:17
  204.3 20.0 %copy-start.3 = (bf16[14336,896]{1,0:T(8,128)(2,1)S(1)}, bf16[14336,896]{1,0:T(8,128)(2,1)}, u32[]{:S(2)}) copy-start(bf16[14336,896]{1,0:T(8,128)(2,1)} %all-gather.4.cloned.1.call-done) | copy-start | bytes 77070336
  261.4 39.4 %copy-start.1 = (bf16[4096,256]{1,0:T(8,128)(2,1)S(1)}, bf16[4096,256]{1,0:T(8,128)(2,1)}, u32[]{:S(2)}) copy-start(bf16[4096,256]{1,0:T(8,128)(2,1)} %param.13) | copy-start | bytes 6291460
Sparse Core Ops, SparseCore 0:
  9.1 59.5 all-gather.7
  70.3 133.9 all-gather.3
  206.0 52.8 all-gather.5
where the time goes:
time: 308 us; the launch traced here: 307 us
  waiting for transfers between devices  170 us (55%)
  matrix products  85.1 us (28%)
  blocking collectives  14 us (5%)
  between operations  13.8 us (4%)
  local copies, waits for them, and re-layouts  10.4 us (3%)
  starting transfers between devices  7.9 us (3%)
  other arithmetic  6.48 us (2%)
    all_gather x1, waiting for transfers between devices, per_device(): pieces = lax.all_gather(output_basis, 'dp', axis=0, tiled=True)  122 us
    dot_general x16, matrix products, per_device(): jnp.dot(grad_cols, pieces[member * shard_rows:(member + 1) * shard_rows],...  57.1 us
    all_gather x1, waiting for transfers between devices, per_device(): right_part = lax.all_gather(query_right, 'dp', axis=0, tiled=True)  46 us
    dot_general x1, matrix products, per_device(): jnp.einsum('ri,dij->drj', left_rows, conditioned, preferred_element_type=...  24.7 us
    all_to_all x1, blocking collectives, from_everyone(): lax.all_to_all(jnp.broadcast_to(array[None], (length, *array.shape)), axi...  14 us
    convert_element_type x1, local copies, waits for them, and re-layouts, per_device(): right_part.reshape(number * rank_rows, right_part.shape[2])  8.68 us
    all_to_all x1, starting transfers between devices, from_everyone(): lax.all_to_all(jnp.broadcast_to(array[None], (length, *array.shape)), axi...  7.83 us
  transfers between devices with their start and end apart: 4, of which 2 were waited for; matrix products, arithmetic and copies ran while one was open for 25% of the time, Pallas kernels for 0%

commit v1 on v0

--- a/solution.py
+++ b/solution.py
@@ -56,7 +56,9 @@
     rotated_in = gather_directly(rotated_share, "mp", 1)
     empty = jnp.zeros((tok_rows, out_cols), jnp.float32)
     running = empty
-    pieces = lax.all_gather(output_basis, "dp", axis=0, tiled=True)
+    pieces = jnp.concatenate(
+        lax.all_to_all(jnp.stack([output_basis] * lax.axis_size("dp")), "dp", 0, 0), axis=0
+    )
     for member in range(pieces.shape[0] // shard_rows):
         grad_cols = lax.dynamic_slice_in_dim(out_grads, member * shard_rows, shard_rows, 1)
         partial_value = jnp.dot(

time: 308 us -> 603 us (1.96)
  waiting for transfers between devices: 170 us -> 442 us
  local copies, waits for them, and re-layouts: 10.4 us -> 20.6 us
  starting transfers between devices: 7.9 us -> 17.5 us
    all_gather x1, waiting for transfers between devices: 46 us -> 286 us  [per_device(): right_part = lax.all_gather(query_right, 'dp', axis=0, tiled=True)]
    all_to_all x0 -> x1, waiting for transfers between devices: none -> 155 us  [per_device(): lax.all_to_all(jnp.stack([output_basis] * lax.axis_size('dp')), 'dp', 0, 0)]
    all_gather x1 -> x0, waiting for transfers between devices: 122 us -> none  [per_device(): pieces = lax.all_gather(output_basis, 'dp', axis=0, tiled=True)]
    another operation x0 -> x1, local copies, waits for them, and re-layouts: none -> 10.1 us  [per_device(): jnp.stack([output_basis] * lax.axis_size('dp'))]
    all_to_all x0 -> x1, starting transfers between devices: none -> 6.06 us  [per_device(): lax.all_to_all(jnp.stack([output_basis] * lax.axis_size('dp')), 'dp', 0, 0)]
  transfers between devices with their start and end apart: 4 -> 4, of which waited for: 2 -> 2; matrix products, arithmetic and copies ran while one was open for 25% -> 13% of each run, Pallas kernels for 0% -> 0%
where the time goes in v1:
time: 603 us
  waiting for transfers between devices  442 us (73%)
  matrix products  86.8 us (14%)
  local copies, waits for them, and re-layouts  20.6 us (3%)
  starting transfers between devices  17.5 us (3%)
  blocking collectives  14.7 us (2%)
  between operations  14.2 us (2%)
  other arithmetic  6.43 us (1%)
    all_gather x1, waiting for transfers between devices, per_device(): right_part = lax.all_gather(query_right, 'dp', axis=0, tiled=True)  286 us
    all_to_all x1, waiting for transfers between devices, per_device(): lax.all_to_all(jnp.stack([output_basis] * lax.axis_size('dp')), 'dp', 0, 0)  155 us
    dot_general x16, matrix products, per_device(): jnp.dot(grad_cols, pieces[member * shard_rows:(member + 1) * shard_rows],...  58.7 us
    dot_general x1, matrix products, per_device(): jnp.einsum('ri,dij->drj', left_rows, conditioned, preferred_element_type=...  24.6 us
    all_to_all x1, blocking collectives, from_everyone(): lax.all_to_all(jnp.broadcast_to(array[None], (length, *array.shape)), axi...  14.7 us
  transfers between devices with their start and end apart: 4, of which 2 were waited for; matrix products, arithmetic and copies ran while one was open for 13% of the time, Pallas kernels for 0%

profile of v1, /device:TPU:0, one launch (start us, length us, event | category | flops | bytes accessed | tf_op | source)
XLA Modules:
  0.0 602.5 jit_solution(15030049772710823454)
XLA Ops:
  6.5 0.0 copy-start
  6.5 10.1 %stack.2 = bf16[16,896,896]{2,1,0:T(8,128)(2,1)} broadcast(bf16[896,896]{1,0:T(8,128)(2,1)} %param.14), dimensions={1,2} | broadcast | bytes 27295744 | tf_op jit(solution)/shard_map/stack | solution.py:60
  16.7 6.1 %all-to-all-start.1 = ((bf16[16,896,896]{2,1,0:T(8,128)(2,1)}), bf16[16,896,896]{2,1,0:T(8,128)(2,1)}, u32[]{:S(2)}, u32[]{:S(2)}) async-start(bf16[16,896,896]{2,1,0:T(8,128)(2,1)} %stack.2), calls=%async_computation.1 | async-start | bytes 51380224 | tf_op jit(solution)/shard_map/all_to_all | solution.py:60
  22.7 0.0 all-gather.5.cloned.1.call-start
  22.8 0.7 all-gather.5.cloned.1.call-update
  23.5 0.0 all-gather.3.cloned.1.call-start
  23.5 0.7 all-gather.3.cloned.1.call-update
  24.9 0.0 copy-done
  24.9 0.0 copy-start.2
  24.9 3.4 convolution_convert_fusion
  28.3 0.1 copy.17
  28.5 0.0 copy-done.2
  28.5 0.3 convert_reduce_fusion
  28.8 285.6 %all-gather.5.cloned.1.call-done = bf16[64,32,896]{2,1,0:T(8,128)(2,1)} async-done(((bf16[4,32,896]{2,1,0:T(8,128)(2,1)}), bf16[64,32,896]{2,1,0:T(8,128)(2,1)}) %all-gather.5.cloned.1.call-update) | async-done | bytes 3670032 | tf_op jit(solution)/shard_map/all_gather | solution.py:82
  314.4 5.5 bitcast_convert_fusion
  319.9 8.7 %copy.18 = f32[1,2048,896]{1,2,0:T(8,128)} copy(f32[1,2048,896]{2,1,0:T(8,128)} %bitcast_convert_fusion) | data formatting | bytes 14680064 | tf_op jit(solution)/shard_map/convert_element_type | solution.py:85
  328.6 155.4 %all-to-all-done.1 = bf16[16,896,896]{2,1,0:T(8,128)(2,1)} async-done(((bf16[16,896,896]{2,1,0:T(8,128)(2,1)}), bf16[16,896,896]{2,1,0:T(8,128)(2,1)}, u32[]{:S(2)}, u32[]{:S(2)}) %all-to-all-start.1) | async-done | bytes 25690144 | tf_op jit(solution)/shard_map/all_to_all | solution.py:60
  484.0 1.6 broadcast_in_dim.7
  485.5 11.4 %all-to-all-start = ((bf16[8,512,256]{1,2,0:T(8,128)(2,1)}), bf16[8,512,256]{1,2,0:T(8,128)(2,1)}, u32[]{:S(2)}, u32[]{:S(2)}) async-start(bf16[8,512,256]{1,2,0:T(8,128)(2,1)} %broadcast_in_dim.7), calls=%async_computation | async-start | bytes 4194304 | tf_op jit(solution)/shard_map/all_to_all | solution.py:17
  496.9 0.0 slice-start
  496.9 3.1 fusion.20
  500.0 0.0 slice-start.1
  500.0 4.0 fusion.21
  504.0 3.8 fusion.22
  507.9 4.0 fusion.23
  511.9 4.0 fusion.24
  515.9 3.8 fusion.25
  519.7 0.0 slice-done
  519.7 0.0 slice-done.1
  519.7 0.0 slice-done.2
  519.7 0.0 slice-done.3
  519.7 3.6 fusion.26
  523.3 3.6 fusion.27
  526.9 3.6 fusion.28
  530.5 3.5 fusion.29
  534.0 3.6 fusion.30
  537.6 3.6 fusion.31
  541.2 3.8 fusion.32
  544.9 3.6 fusion.33
  548.5 3.6 fusion.34
  552.1 3.6 fusion.35
  555.7 0.0 all-to-all-done
  555.7 24.6 %fusion = f32[2048]{0:T(1024)S(1)} fusion(f32[1,2048,896]{1,2,0:T(8,128)} %copy.18, bf16[2048,2048]{1,0:T(8,128)(2,1)} %bitcast.109, bf16[2048,896]{1,0:T(8,128)(2,1)} %param.15, bf16[512,2048]{0,1:T(8,128)(2,1)} %bitcast.1, f32[512]{0:T(512)S(1)} %divide_select_fusion, bf16[512,896]{1,0:T(8,128)(2,1)} %fusion.35, bf16[512,896]{1,0:T(8,128)(2,1)} %fusion.34, ...), kind=kOutput, calls=%fused_computation.1 | convolution fusion | flops 9422305280 | bytes 36186112 | tf_op jit(solution)/shard_map/ri,dij->drj/dot_general | solution.py:86
  580.3 0.1 reduce_sum.38
  580.4 0.1 reduce_sum.39
  580.5 14.7 %all_to_all.15 = f32[8,1,64]{2,1,0:T(1,128)S(1)} all-to-all(f32[8,1,64]{2,1,0:T(1,128)S(1)} %broadcast_in_dim.9), channel_id=1, replica_groups=mesh['dp'=16,'mp'=8] {'mp'}, dimensions={0} | all-to-all | bytes 4096 | tf_op jit(solution)/shard_map/all_to_all | solution.py:17
  595.2 0.5 reduce_sum.40
  595.7 0.0 copy-done.1
  (8 shorter events, 0.0 us)
Async XLA Ops:
  6.5 18.3 %copy-start = (bf16[4096,256]{1,0:T(8,128)(2,1)S(1)}, bf16[4096,256]{1,0:T(8,128)(2,1)}, u32[]{:S(2)}) copy-start(bf16[4096,256]{1,0:T(8,128)(2,1)} %param.13) | copy-start | bytes 6291460
  16.7 467.3 %all-to-all-start.1 = ((bf16[16,896,896]{2,1,0:T(8,128)(2,1)}), bf16[16,896,896]{2,1,0:T(8,128)(2,1)}, u32[]{:S(2)}, u32[]{:S(2)}) async-start(bf16[16,896,896]{2,1,0:T(8,128)(2,1)} %stack.2), calls=%async_computation.1 | async-start | bytes 51380224 | tf_op jit(solution)/shard_map/all_to_all | solution.py:60
  22.7 291.7 %all-gather.5.cloned.1.call-start = ((), (), s32[]{:S(2)}) async-start(), calls=%async_computation.4 | async-start | bytes 3899392 | tf_op jit(solution)/shard_map/all_gather | solution.py:82
  23.5 532.2 %all-gather.3.cloned.1.call-start = ((), (), s32[]{:S(2)}) async-start(), calls=%async_computation.3 | async-start | bytes 8912896 | tf_op jit(solution)/shard_map/all_gather | solution.py:81
  24.9 3.6 copy-start.2
  485.5 70.1 %all-to-all-start = ((bf16[8,512,256]{1,2,0:T(8,128)(2,1)}), bf16[8,512,256]{1,2,0:T(8,128)(2,1)}, u32[]{:S(2)}, u32[]{:S(2)}) async-start(bf16[8,512,256]{1,2,0:T(8,128)(2,1)} %broadcast_in_dim.7), calls=%async_computation | async-start | bytes 4194304 | tf_op jit(solution)/shard_map/all_to_all | solution.py:17
  496.9 22.8 %slice-start = ((s8[14680064]{0:T(1024)(128)(4,1)}), s8[4194304]{0:T(1024)(128)(4,1)S(1)}, s32[]{:S(2)}) async-start(s8[14680064]{0:T(1024)(128)(4,1)} %bitcast.107), calls=%async_computation.5 | async-start | bytes 8388608
  500.0 19.7 %slice-start.1 = ((s8[14680064]{0:T(1024)(128)(4,1)}), s8[4194304]{0:T(1024)(128)(4,1)S(1)}, s32[]{:S(2)}) async-start(s8[14680064]{0:T(1024)(128)(4,1)} %bitcast.107), calls=%async_computation.6 | async-start | bytes 8388608
  507.9 11.8 %slice-start.2 = ((s8[14680064]{0:T(1024)(128)(4,1)}), s8[4194304]{0:T(1024)(128)(4,1)S(1)}, s32[]{:S(2)}) async-start(s8[14680064]{0:T(1024)(128)(4,1)} %bitcast.107), calls=%async_computation.7 | async-start | bytes 8388608
  511.9 7.8 %slice-start.3 = ((s8[14680064]{0:T(1024)(128)(4,1)}), s8[2097152]{0:T(1024)(128)(4,1)S(1)}, s32[]{:S(2)}) async-start(s8[14680064]{0:T(1024)(128)(4,1)} %bitcast.107), calls=%async_computation.8 | async-start | bytes 4194304
  555.7 40.0 %copy-start.1 = (bf16[4096,256]{1,0:T(8,128)(2,1)S(1)}, bf16[4096,256]{1,0:T(8,128)(2,1)}, u32[]{:S(2)}) copy-start(bf16[4096,256]{1,0:T(8,128)(2,1)} %param.13) | copy-start | bytes 6291460
Sparse Core Ops, SparseCore 0:
  25.3 289.1 all-gather.4
  316.1 116.3 all-gather.2
